TPU v7x, 512 devices: a whole 4x4x16 slice. The times are simulated.
512 devices in a mesh: tile: 128 (over z, y, core), fac: 4 (over x).
Axes of the slice: x: 4, y: 4, z: 16, core: 2. Of those that a mesh axis runs over, the one named last changes fastest.
Arguments:
- panel: float32 [64, 1024, 2048], P('fac', 'tile'), may hold values from -7000 to 7000
- materials: int32 [1024, 2048], P('tile'), may hold values from 0 to 7
- table: float32 [4, 8], replicated, may hold values from 0.2 to 5
- shifts: float32 [8], replicated, may hold values from 0.05 to 0.5
- shift_pick: int32 [1], replicated, may hold values from 0 to 7
Outputs:
- basis: float32 [64, 1024, 2048], P('fac', 'tile')
All inputs are finite; a program needn't handle non-finite values.
Results may differ from a plain program's by a relative error of at most 0.0003.
Values sent between devices are 32-bit elements; how exact they have to be, the bound alone decides.
A program may use at most 64 MiB of HBM per device.

v0:
```python
import jax
import jax.numpy as jnp
from jax import lax
from jax.sharding import PartitionSpec as P

NZ = 64
SWEEPS = 4


OMEGA = 0.8


def padded(value, sides, width):
    for axis, dim in sides:
        count, length = (lax.axis_size(axis), value.shape[dim])
        up = [(i, (i + 1) % count) for i in range(count - 1)]
        down = [(j, i) for i, j in up]
        last = lax.slice_in_dim(value, length - width, length, axis=dim)
        initial = lax.slice_in_dim(value, 0, width, axis=dim)
        before = lax.ppermute(last, axis, up)
        after = lax.ppermute(initial, axis, down)
        value = jnp.concatenate([before, value, after], axis=dim)
    return value


def swapped(value, axis, apart):
    return lax.ppermute(value, axis, [(i, i ^ 1 << apart) for i in range(lax.axis_size(axis))])


def harmonic(first, second):
    total = first + second
    safe = jnp.where(total > 0, total, 1.0)
    return 2.0 * first * second / safe


def material_fields(materials, table):
    fields = jnp.zeros((4,) + materials.shape, jnp.float32)
    for index in range(table.shape[1]):
        fields = fields + jnp.where(materials[None] == index, table[:, index][:, None, None], 0.0)
    return fields


def coefficients(fields, shift_value):
    cond_x = fields[0]
    faces_x = harmonic(cond_x[:-1], cond_x[1:])
    prev_x = faces_x[:-1]
    next_x = faces_x[1:]
    inner = fields[:, 1:-1]
    cond_y = inner[1]
    cond_z = inner[2]
    capacity = inner[3]
    count = cond_y.shape[0]
    width = cond_y.shape[1]
    zeros_y = jnp.zeros((count, NZ), jnp.float32)
    zeros_z = jnp.zeros((count, 1), jnp.float32)
    upper_y = jnp.concatenate([cond_y[:, NZ:], zeros_y], 1)
    next_y = harmonic(cond_y, upper_y)
    prev_y = jnp.concatenate([zeros_y, next_y[:, :-NZ]], 1)
    layer = jnp.arange(width) % NZ
    upper_z = jnp.concatenate([cond_z[:, 1:], zeros_z], 1)
    upper_z = jnp.where(layer[None] < NZ - 1, upper_z, 0.0)
    next_z = harmonic(cond_z, upper_z)
    prev_z = jnp.concatenate([zeros_z, next_z[:, :-1]], 1)
    diagonal = shift_value * capacity + prev_x + next_x + prev_y + next_y + prev_z + next_z
    inverse = jnp.where(capacity > 0, 1.0 / jnp.where(capacity > 0, diagonal, 1.0), 0.0)
    return (prev_x, next_x, prev_y, next_y, prev_z, next_z, inverse)


def relax(extended, source, coeffs):
    prev_x, next_x, prev_y, next_y, prev_z, next_z, inverse = coeffs
    center = extended[:, 1:-1]
    shape_y = center.shape[:-1] + (NZ,)
    shape_z = center.shape[:-1] + (1,)
    up_y = jnp.concatenate([center[..., NZ:], jnp.zeros(shape_y, center.dtype)], -1)
    down_y = jnp.concatenate([jnp.zeros(shape_y, center.dtype), center[..., :-NZ]], -1)
    up_z = jnp.concatenate([center[..., 1:], jnp.zeros(shape_z, center.dtype)], -1)
    down_z = jnp.concatenate([jnp.zeros(shape_z, center.dtype), center[..., :-1]], -1)
    beside = prev_x * extended[:, :-2] + next_x * extended[:, 2:]
    beside = beside + next_y * up_y + prev_y * down_y + next_z * up_z + prev_z * down_z
    return (1.0 - OMEGA) * center + OMEGA * (source + beside) * inverse


def gram_of(matrix):
    return jnp.dot(
        matrix, matrix.T, precision=lax.Precision.HIGHEST, preferred_element_type=jnp.float32
    )


def per_device(panel, materials, table, shifts, shift_pick):
    picker = jnp.arange(shifts.shape[0]) == shift_pick[0]
    shift_value = jnp.sum(jnp.where(picker, shifts, 0.0))
    fields = material_fields(materials, table)
    fields_ext = padded(fields, (("tile", 1),), 1)
    coeffs = coefficients(fields_ext, shift_value)
    solution = panel * coeffs[6][None]
    for sweep_index in range(SWEEPS):
        extended = padded(solution, (("tile", 1),), 1)
        solution = relax(extended, panel, coeffs)
    own_cols = solution.shape[0]
    column_count = 2 * own_cols
    ncells = solution.shape[1] * lax.axis_size("tile") * solution.shape[2]
    position = lax.axis_index("fac")
    half_id = position % 2
    half_rows = solution.shape[1] // 2
    keeping = lax.dynamic_slice_in_dim(solution, half_id * half_rows, half_rows, 1)
    giving = lax.dynamic_slice_in_dim(solution, (1 - half_id) * half_rows, half_rows, 1)
    received = swapped(giving, "fac", 0)
    merged = jnp.where(
        half_id == 0,
        jnp.concatenate([keeping, received], 0),
        jnp.concatenate([received, keeping], 0),
    )
    matrix = merged.reshape(column_count, -1)
    partial_value = gram_of(matrix)
    tile_sum = lax.psum(partial_value, "tile")
    total = tile_sum + swapped(tile_sum, "fac", 0)
    lower_factor = jnp.linalg.cholesky(total / ncells)
    ortho = lax.linalg.triangular_solve(lower_factor, matrix, left_side=True, lower=True).reshape(
        merged.shape
    )
    mine = lax.dynamic_slice_in_dim(ortho, half_id * own_cols, own_cols, 0)
    theirs = lax.dynamic_slice_in_dim(ortho, (1 - half_id) * own_cols, own_cols, 0)
    returned = swapped(theirs, "fac", 0)
    result = jnp.where(
        half_id == 0, jnp.concatenate([mine, returned], 1), jnp.concatenate([returned, mine], 1)
    )
    return result


def solution(mesh):
    placed = (P("fac", "tile", None), P("tile", None), P(), P(), P())
    return jax.shard_map(
        per_device, mesh=mesh, in_specs=placed, out_specs=P("fac", "tile", None), check_vma=False
    )
```

profile of v0, /device:TPU:6, one launch (start us, length us, event | category | flops | bytes accessed | tf_op | source)
XLA Modules:
  0.0 592.4 jit_solution(5284592554948806002)
XLA Ops:
  1.6 1.7 collective-permute-start
  6.3 1.5 collective-permute-done.1
  9.6 4.5 collective-permute-start.2
  15.8 1.6 collective-permute-done.3
  17.4 1.6 fusion.41
  19.4 5.0 collective-permute-start.4
  26.1 1.6 collective-permute-done.5
  27.6 1.6 fusion.31
  29.7 5.0 collective-permute-start.6
  36.3 1.6 collective-permute-done.7
  37.9 1.6 fusion.21
  39.9 6.6 %collective-permute-start.8 = (f32[16,1,2048]{2,0,1:T(8,128)S(1)}, f32[16,1,2048]{2,0,1:T(8,128)S(1)}, u32[]{:S(2)}, u32[]{:S(2)}) collective-permute-start(f32[16,1,2048]{2,0,1:T(8,128)S(1)} %get-tuple-element.23), channel_id=1, source_target_pairs={{0,4},{4,8},{8,12},{12,16},{16,20},{20,24},{24,28},{28,32},{32,36}... | collective-permute-start | bytes 393224 | tf_op jit(solution)/shard_map/ppermute | solution.py:20
  48.1 1.6 collective-permute-done.9
  49.7 1.6 fusion.11
  51.4 2.9 collective-permute-start.10
  54.4 9.4 %collective-permute-done.10 = f32[16,4,2048]{2,0,1:T(8,128)S(1)} collective-permute-done((f32[16,4,2048]{2,0,1:T(8,128)S(1)}, f32[16,4,2048]{2,0,1:T(8,128)S(1)}, u32[]{:S(2)}, u32[]{:S(2)}) %collective-permute-start.10) | collective-permute-done | bytes 524320 | tf_op jit(solution)/shard_map/ppermute | solution.py:27
  64.8 501.3 %psum.7 = f32[32,32]{0,1:T(8,128)S(1)} all-reduce(f32[32,32]{0,1:T(8,128)S(1)} %convolution_bitcast_fusion), channel_id=1, replica_groups=mesh['tile'=128,'fac'=4] {'tile'}, use_global_device_ids=true, to_apply=%region_1.2 | all-reduce | flops 1024 | bytes 8192 | tf_op jit(solution)/shard_map/psum | solution.py:115
  566.1 2.7 collective-permute-start.11
  568.9 2.8 collective-permute-done.11
  571.8 2.9 cholesky.16
  576.0 2.4 custom-call.6
  579.6 2.7 collective-permute-start.12
  582.4 8.3 %collective-permute-done.12 = f32[16,4,2048]{2,0,1:T(8,128)S(1)} collective-permute-done((f32[16,4,2048]{2,0,1:T(8,128)S(1)}, f32[16,4,2048]{2,0,1:T(8,128)S(1)}, u32[]{:S(2)}, u32[]{:S(2)}) %collective-permute-start.12) | collective-permute-done | bytes 524320 | tf_op jit(solution)/shard_map/ppermute | solution.py:27
  590.8 1.6 copy.30
  (55 shorter events, 17.0 us)
Async XLA Ops:
  0.0 0.9 copy-start.1
  1.6 4.7 collective-permute-start
  3.3 4.5 collective-permute-start.1
  4.6 1.0 copy-start.2
  4.7 3.9 copy-start
  9.6 6.2 %collective-permute-start.2 = (f32[16,1,2048]{2,0,1:T(8,128)S(1)}, f32[16,1,2048]{2,0,1:T(8,128)S(1)}, u32[]{:S(2)}, u32[]{:S(2)}) collective-permute-start(f32[16,1,2048]{2,0,1:T(8,128)S(1)} %get-tuple-element.41), channel_id=1, source_target_pairs={{0,4},{4,8},{8,12},{12,16},{16,20},{20,24},{24,28},{28,32},{32,36}... | collective-permute-start | bytes 393224 | tf_op jit(solution)/shard_map/ppermute | solution.py:20
  14.1 3.2 collective-permute-start.3
  19.4 6.7 %collective-permute-start.4 = (f32[16,1,2048]{2,0,1:T(8,128)S(1)}, f32[16,1,2048]{2,0,1:T(8,128)S(1)}, u32[]{:S(2)}, u32[]{:S(2)}) collective-permute-start(f32[16,1,2048]{2,0,1:T(8,128)S(1)} %get-tuple-element.35), channel_id=1, source_target_pairs={{0,4},{4,8},{8,12},{12,16},{16,20},{20,24},{24,28},{28,32},{32,36}... | collective-permute-start | bytes 393224 | tf_op jit(solution)/shard_map/ppermute | solution.py:20
  24.4 3.2 collective-permute-start.5
  29.7 6.6 %collective-permute-start.6 = (f32[16,1,2048]{2,0,1:T(8,128)S(1)}, f32[16,1,2048]{2,0,1:T(8,128)S(1)}, u32[]{:S(2)}, u32[]{:S(2)}) collective-permute-start(f32[16,1,2048]{2,0,1:T(8,128)S(1)} %get-tuple-element.29), channel_id=1, source_target_pairs={{0,4},{4,8},{8,12},{12,16},{16,20},{20,24},{24,28},{28,32},{32,36}... | collective-permute-start | bytes 393224 | tf_op jit(solution)/shard_map/ppermute | solution.py:20
  34.6 3.2 collective-permute-start.7
  39.9 8.2 %collective-permute-start.8 = (f32[16,1,2048]{2,0,1:T(8,128)S(1)}, f32[16,1,2048]{2,0,1:T(8,128)S(1)}, u32[]{:S(2)}, u32[]{:S(2)}) collective-permute-start(f32[16,1,2048]{2,0,1:T(8,128)S(1)} %get-tuple-element.23), channel_id=1, source_target_pairs={{0,4},{4,8},{8,12},{12,16},{16,20},{20,24},{24,28},{28,32},{32,36}... | collective-permute-start | bytes 393224 | tf_op jit(solution)/shard_map/ppermute | solution.py:20
  46.4 3.2 collective-permute-start.9
  51.4 12.4 %collective-permute-start.10 = (f32[16,4,2048]{2,0,1:T(8,128)S(1)}, f32[16,4,2048]{2,0,1:T(8,128)S(1)}, u32[]{:S(2)}, u32[]{:S(2)}) collective-permute-start(f32[16,4,2048]{2,0,1:T(8,128)S(1)} %get-tuple-element.18), channel_id=1, source_target_pairs={{0,1},{1,0},{2,3},{3,2},{4,5},{5,4},{6,7},{7,6},{8,9},{9,8},{10,11... | collective-permute-start | bytes 1572872 | tf_op jit(solution)/shard_map/ppermute | solution.py:27
  566.1 5.6 collective-permute-start.11
  579.6 11.1 %collective-permute-start.12 = (f32[16,4,2048]{2,0,1:T(8,128)S(1)}, f32[16,4,2048]{2,0,1:T(8,128)S(1)}, u32[]{:S(2)}, u32[]{:S(2)}) collective-permute-start(f32[16,4,2048]{2,0,1:T(8,128)S(1)} %get-tuple-element.16), channel_id=1, source_target_pairs={{0,1},{1,0},{2,3},{3,2},{4,5},{5,4},{6,7},{7,6},{8,9},{9,8},{10,11... | collective-permute-start | bytes 1572872 | tf_op jit(solution)/shard_map/ppermute | solution.py:27
where the time goes:
time: 603 us; the launch traced here: 592 us
  blocking collectives  501 us (83%)
  starting transfers between devices  37.7 us (6%)
  waiting for transfers between devices  28.4 us (5%)
  other arithmetic  16.6 us (3%)
    psum x1, blocking collectives, per_device(): tile_sum = lax.psum(partial_value, 'tile')  501 us
    ppermute x5, starting transfers between devices, padded(): before = lax.ppermute(last, axis, up)  22.8 us
    ppermute x3, waiting for transfers between devices, swapped(): lax.ppermute(value, axis, [(i, i ^ 1 << apart) for i in range(lax.axis_si...  20.5 us
  transfers between devices with their start and end apart: 13, of which 8 were waited for; matrix products, arithmetic and copies ran while one was open for 0% of the time, Pallas kernels for 0%

commit v1 on v0

v1 whole, which is shorter than its diff:
```python
import functools

import jax
import jax.numpy as jnp
from jax import lax
from jax.experimental import pallas as pl
from jax.experimental.pallas import tpu as pltpu
from jax.sharding import PartitionSpec as P

NZ = 64
SWEEPS = 4
OMEGA = 0.8
LANES = 128
YS = 4
CORES = 2
GROUP = 2 * YS * CORES
LINE = YS * CORES
HALO = 4
MESH = pl.DeviceIdType.MESH
HIGHEST = lax.Precision.HIGHEST


def chunked(value):
    return [value[:, i:i + LANES] for i in range(0, value.shape[1], LANES)]


def lane_iota(rows):
    return lax.broadcasted_iota(jnp.int32, (rows, LANES), 1)


def row_iota(rows):
    return lax.broadcasted_iota(jnp.int32, (rows, LANES), 0)


def pick_field(ids, table, field):
    low = (ids & 1) == 1
    mid = (ids & 2) == 2
    high = (ids & 4) == 4
    pairs = [jnp.where(low, table[field, i + 1], table[field, i]) for i in range(0, 8, 2)]
    quads = [jnp.where(mid, pairs[1], pairs[0]), jnp.where(mid, pairs[3], pairs[2])]
    return jnp.where(high, quads[1], quads[0])


def harmonic(first, second):
    return 2.0 * first * second / (first + second)


def make_coefficients(tiles, me, shift_value, ids_ref, table, coef, inv_ref):
    count = ids_ref.shape[1] // LANES
    ids = chunked(ids_ref[...])
    rows24 = row_iota(24)
    cut = ((me == 0) & (rows24 == 7)) | ((me == tiles - 1) & (rows24 == 15))
    lane = lane_iota(16)
    left = lane < NZ
    top = (lane % NZ) == NZ - 1
    cond_y = [pick_field(i[4:20], table, 1) for i in ids]
    turned = [pltpu.roll(v, NZ, 1) for v in cond_y]
    faces_y = []
    for k in range(count):
        above = jnp.where(left, turned[k], turned[min(k + 1, count - 1)])
        face = harmonic(cond_y[k], above)
        if k == count - 1:
            face = jnp.where(left, face, 0.0)
        faces_y.append(face)
    back_y = [pltpu.roll(v, NZ, 1) for v in faces_y]
    for k in range(count):
        below = back_y[k - 1] if k else jnp.zeros_like(back_y[0])
        next_y = faces_y[k]
        prev_y = jnp.where(left, below, back_y[k])
        cond_z = pick_field(ids[k][4:20], table, 2)
        next_z = harmonic(cond_z, pltpu.roll(cond_z, LANES - 1, 1))
        next_z = jnp.where(top, 0.0, next_z)
        prev_z = pltpu.roll(next_z, 1, 1)
        cond_x = pick_field(ids[k], table, 0)
        faces_x = harmonic(cond_x, pltpu.roll(cond_x, 23, 0))
        faces_x = jnp.where(cut, 0.0, faces_x)
        prev_x = faces_x[3:19]
        next_x = faces_x[4:20]
        capacity = pick_field(ids[k][4:20], table, 3)
        diagonal = shift_value * capacity + prev_x + next_x + prev_y + next_y + prev_z + next_z
        inverse = 1.0 / diagonal
        scaled = OMEGA * inverse
        where = pl.ds(k * LANES, LANES)
        for i, face in enumerate((prev_x, next_x, prev_y, next_y, prev_z, next_z)):
            coef[i, :, where] = face * scaled
        inv_ref[:, where] = inverse


def solve_column(source_ref, coef, inv_ref):
    count = inv_ref.shape[1] // LANES
    where = [pl.ds(k * LANES, LANES) for k in range(count)]
    left = lane_iota(16) < NZ
    values = [source_ref[:, where[k]] * inv_ref[:, where[k]] for k in range(count)]
    base = [OMEGA * v for v in values]
    for sweep in range(SWEEPS):
        turned = [pltpu.roll(v, NZ, 1) for v in values]
        new = []
        for k in range(count):
            v = values[k]
            total = (1.0 - OMEGA) * v + base[k]
            total += coef[0, :, where[k]] * pltpu.roll(v, 1, 0)
            total += coef[1, :, where[k]] * pltpu.roll(v, 15, 0)
            below = jnp.where(left, turned[max(k - 1, 0)], turned[k])
            above = jnp.where(left, turned[k], turned[min(k + 1, count - 1)])
            total += coef[2, :, where[k]] * below
            total += coef[3, :, where[k]] * above
            total += coef[4, :, where[k]] * pltpu.roll(v, 1, 1)
            total += coef[5, :, where[k]] * pltpu.roll(v, LANES - 1, 1)
            new.append(total)
        values = new
    return values


def diagonal_blocks(product):
    size = product.shape[0]
    keep = (row_iota(size) % 8) == (lane_iota(size) % 8)
    kept = jnp.where(keep, product, 0.0)
    return jnp.sum(kept.reshape(size // 8, 8, LANES), axis=1)


def pack(blocks):
    source = lax.broadcasted_iota(jnp.int32, (LANES, LANES), 0)
    target = lax.broadcasted_iota(jnp.int32, (LANES, LANES), 1)
    left, right = [], []
    for value, first_row, first_column in blocks:
        for half in range(2):
            left.append(value[half * 8:half * 8 + 8])
            place = (first_row + half * 8) * 4 + first_column + source // 8
            right.append((place == target).astype(jnp.float32))
    total = None
    for a, b in zip(left, right):
        part = jnp.dot(a, b, precision=HIGHEST, preferred_element_type=jnp.float32)
        total = part if total is None else total + part
    return total


def inverse_factor(packed, size):
    lane = lane_iota(8)
    eye_lane = lane_iota(size)
    eye_row = row_iota(size)
    tiles = [packed] + [pltpu.roll(packed, LANES - 32 * q, 1) for q in range(1, size // 8)]
    matrix = jnp.concatenate([jnp.where(lane < size, t, 0.0) for t in tiles], 0)
    matrix = jnp.where(eye_lane == eye_row + size, 1.0, matrix)
    for k in range(size - 1):
        row = matrix[k:k + 1, :]
        column = matrix[:, k:k + 1]
        pivot = 1.0 / matrix[k:k + 1, k:k + 1]
        factor = jnp.where(eye_row > k, column * pivot, 0.0)
        matrix = matrix - factor * row
    diagonal = jnp.sum(jnp.where(eye_lane == eye_row, matrix, 0.0), axis=1, keepdims=True)
    scaled = matrix * (1.0 / jnp.sqrt(diagonal))
    return pltpu.roll(scaled, LANES - size, 1)


def solve_kernel(tiles, panel, ids, table, shifts, pick, w_out, r_out, inv_out, ext, idx, coef, inv_ref, w, r, gbuf, zbuf,
                 ids_sem, own_sem, ids_send, ids_recv, halo_send, halo_recv, swap_send, swap_recv, rest_sem, out_sem,
                 group_send, group_recv, line_send, line_recv):
    cols = panel.shape[0]
    width = panel.shape[2]
    half = width // 2
    zs = tiles // LINE
    me = lax.axis_index("tile")
    fac = lax.axis_index("fac")
    parity = fac % 2
    partner = fac + 1 - 2 * parity
    line = me // LINE
    spot = me % LINE
    before = lax.rem(me + tiles - 1, tiles)
    after = lax.rem(me + 1, tiles)
    seat = parity * LINE + spot

    own_ids = pltpu.make_async_copy(ids, idx.at[pl.ds(8, 8)], ids_sem)
    own_ids.start()
    own_panel = pltpu.make_async_copy(panel, ext.at[:, pl.ds(HALO, 8)], own_sem)
    own_panel.start()

    def group_peer(step):
        there = lax.rem(seat + step, GROUP)
        peer_fac = fac - parity + there // LINE
        return {"tile": line * LINE + there % LINE, "fac": peer_fac}, there

    def line_peer(step):
        there = lax.rem(line + step, zs)
        return {"tile": there * LINE + spot, "fac": fac}, there

    barrier = pltpu.get_barrier_semaphore()
    greeted = [{"tile": before, "fac": fac}, {"tile": after, "fac": fac}]
    greeted += [group_peer(i)[0] for i in range(1, GROUP)]
    greeted += [line_peer(i)[0] for i in range(1, zs)]
    for peer in greeted:
        pl.semaphore_signal(barrier, inc=1, device_id=peer, device_id_type=MESH)
    pl.semaphore_wait(barrier, len(greeted))

    ids_up = pltpu.make_async_remote_copy(ids, idx.at[pl.ds(0, 8)], ids_send.at[0], ids_recv.at[0],
                                          device_id={"tile": after, "fac": fac}, device_id_type=MESH)
    ids_down = pltpu.make_async_remote_copy(ids, idx.at[pl.ds(16, 8)], ids_send.at[1], ids_recv.at[1],
                                            device_id={"tile": before, "fac": fac}, device_id_type=MESH)
    ids_up.start()
    ids_down.start()

    def halo_up(c):
        return pltpu.make_async_remote_copy(panel.at[c, pl.ds(8 - HALO, HALO)], ext.at[c, pl.ds(0, HALO)],
                                            halo_send.at[0, c], halo_recv.at[0, c],
                                            device_id={"tile": after, "fac": fac}, device_id_type=MESH)

    def halo_down(c):
        return pltpu.make_async_remote_copy(panel.at[c, pl.ds(0, HALO)], ext.at[c, pl.ds(8 + HALO, HALO)],
                                            halo_send.at[1, c], halo_recv.at[1, c],
                                            device_id={"tile": before, "fac": fac}, device_id_type=MESH)

    def send_halo(c, carry):
        halo_up(c).start()
        halo_down(c).start()
        return carry

    lax.fori_loop(0, cols, send_halo, 0)

    giving = pl.ds(pl.multiple_of(parity * half, half), half)
    getting = pl.ds(pl.multiple_of((1 - parity) * half, half), half)

    def swap(c):
        return pltpu.make_async_remote_copy(w.at[c, :, giving], r.at[c, :, giving], swap_send.at[c], swap_recv.at[c],
                                            device_id={"tile": me, "fac": partner}, device_id_type=MESH)

    shift_value = shifts[pick[0]]
    own_ids.wait()
    ids_up.wait()
    ids_down.wait()
    make_coefficients(tiles, me, shift_value, idx, table, coef, inv_ref)
    own_panel.wait()

    def column(c, carry):
        halo_up(c).wait()
        halo_down(c).wait()

        @pl.when(c > 0)
        def _():
            swap(c - 1).start()

        values = solve_column(ext.at[c], coef, inv_ref)
        for k, value in enumerate(values):
            w[c, :, pl.ds(k * LANES, LANES)] = value[HALO:HALO + 8]
        return carry

    lax.fori_loop(0, cols, column, 0)
    own = w[...].reshape(cols * 8, width)
    gram = lax.dot_general(own, own, (((1,), (1,)), ((), ())), precision=HIGHEST, preferred_element_type=jnp.float32)
    swap(cols - 1).start()
    own_blocks = diagonal_blocks(gram)
    keep_w = pltpu.make_async_copy(w, w_out, out_sem.at[0])
    keep_w.start()

    def arrived(c, carry):
        swap(c).wait()
        return carry

    lax.fori_loop(0, cols, arrived, 0)
    keep_r = pltpu.make_async_copy(r.at[:, :, getting], r_out.at[:, :, getting], out_sem.at[1])
    keep_r.start()
    mine = w[:, :, getting].reshape(cols * 8, half)
    theirs = r[:, :, getting].reshape(cols * 8, half)
    cross = lax.dot_general(mine, theirs, (((1,), (1,)), ((), ())), precision=HIGHEST, preferred_element_type=jnp.float32)
    across = lax.dot_general(theirs, mine, (((1,), (1,)), ((), ())), precision=HIGHEST, preferred_element_type=jnp.float32)
    mine_at = parity * cols
    theirs_at = cols - mine_at
    gbuf[seat] = pack([(own_blocks, mine_at, mine_at), (diagonal_blocks(cross), mine_at, theirs_at),
                       (diagonal_blocks(across), theirs_at, mine_at)])

    def group_copy(step):
        peer, _ = group_peer(step)
        return pltpu.make_async_remote_copy(gbuf.at[seat], gbuf.at[seat], group_send.at[step], group_recv.at[seat],
                                            device_id=peer, device_id_type=MESH)

    def group_arrival(step):
        peer, there = group_peer(step)
        return pltpu.make_async_remote_copy(gbuf.at[there], gbuf.at[there], group_send.at[step], group_recv.at[there],
                                            device_id=peer, device_id_type=MESH)

    def line_copy(step):
        peer, _ = line_peer(step)
        return pltpu.make_async_remote_copy(zbuf.at[line], zbuf.at[line], line_send.at[step], line_recv.at[line],
                                            device_id=peer, device_id_type=MESH)

    def line_arrival(step):
        peer, there = line_peer(step)
        return pltpu.make_async_remote_copy(zbuf.at[there], zbuf.at[there], line_send.at[step], line_recv.at[there],
                                            device_id=peer, device_id_type=MESH)

    rest = pltpu.make_async_remote_copy(w.at[:, :, pl.ds(half, half)], r_out.at[:, :, pl.ds(half, half)],
                                        rest_sem.at[0], rest_sem.at[1],
                                        device_id={"tile": me, "fac": partner}, device_id_type=MESH)
    for step in range(1, GROUP):
        group_copy(step).start()

    @pl.when(parity == 0)
    def _():
        rest.start()

    for step in range(1, GROUP):
        group_arrival(step).wait_recv()
    total = gbuf[0]
    for i in range(1, GROUP):
        total = total + gbuf[i]
    zbuf[line] = total
    order = sorted(range(1, zs), key=lambda s: -min(s, zs - s))
    for step in order:
        line_copy(step).start()
    for step in range(1, zs):
        line_arrival(step).wait_recv()
    total = zbuf[0]
    for i in range(1, zs):
        total = total + zbuf[i]
    cells = 8 * tiles * width
    inv_out[...] = inverse_factor(total / cells, 2 * cols)

    for step in range(1, GROUP):
        group_copy(step).wait_send()
    for step in range(1, zs):
        line_copy(step).wait_send()
    keep_w.wait()
    keep_r.wait()

    @pl.when(parity == 0)
    def _():
        rest.wait_send()

    @pl.when(parity == 1)
    def _():
        rest.wait_recv()


def split(value):
    high = value.astype(jnp.bfloat16)
    low = (value - high.astype(jnp.float32)).astype(jnp.bfloat16)
    return high, low


def dot3(a, b):
    ah, al = a
    bh, bl = b
    first = jnp.dot(ah, bh, preferred_element_type=jnp.float32)
    second = jnp.dot(ah, bl, preferred_element_type=jnp.float32)
    third = jnp.dot(al, bh, preferred_element_type=jnp.float32)
    return first + (second + third)


def apply_kernel(cols, inv, w, r, out, own_high, own_low, rec_high, rec_low):
    parity = lax.axis_index("fac") % 2

    @pl.when(pl.program_id(0) == 0)
    def _():
        rows = jnp.where(parity == 0, inv[0:cols, :], inv[cols:2 * cols, :])
        rows = jnp.broadcast_to(rows[:, None, :], (cols, 8, LANES)).reshape(cols * 8, LANES)
        high, low = split(rows)
        source = row_iota(LANES)
        target = lane_iota(LANES)
        same = (source % 8) == (target % 8)
        for first, ref_high, ref_low in ((parity * cols, own_high, own_low), (0, rec_high, rec_low)):
            spread = (source == first + target // 8).astype(jnp.bfloat16)
            for value, ref in ((high, ref_high), (low, ref_low)):
                wide = jnp.dot(value, spread, preferred_element_type=jnp.float32)
                ref[...] = jnp.where(same, wide, 0.0).astype(jnp.bfloat16)

    out[...] = dot3((own_high[...], own_low[...]), split(w[...]))

    @pl.when(parity == 1)
    def _():
        out[...] += dot3((rec_high[...], rec_low[...]), split(r[...]))


def per_device(tiles, panel, materials, table, shifts, shift_pick):
    cols, depth, width = panel.shape
    zs = tiles // LINE
    anywhere = pl.BlockSpec(memory_space=pl.ANY)
    scalars = pl.BlockSpec(memory_space=pltpu.SMEM)
    dma = pltpu.SemaphoreType.DMA
    f32 = jnp.float32
    w, r, inv = pl.pallas_call(
        functools.partial(solve_kernel, tiles),
        name="solve",
        out_shape=(jax.ShapeDtypeStruct((cols, depth, width), f32), jax.ShapeDtypeStruct((cols, depth, width), f32),
                   jax.ShapeDtypeStruct((2 * cols, LANES), f32)),
        in_specs=[anywhere, anywhere, scalars, scalars, scalars],
        out_specs=(anywhere, anywhere, pl.BlockSpec(memory_space=pltpu.VMEM)),
        scratch_shapes=[
            pltpu.VMEM((cols, 16, width), f32),
            pltpu.VMEM((24, width), jnp.int32),
            pltpu.VMEM((6, 16, width), f32),
            pltpu.VMEM((16, width), f32),
            pltpu.VMEM((cols, depth, width), f32),
            pltpu.VMEM((cols, depth, width), f32),
            pltpu.VMEM((GROUP, 8, LANES), f32),
            pltpu.VMEM((zs, 8, LANES), f32),
            dma, dma, dma((2,)), dma((2,)), dma((2, cols)), dma((2, cols)), dma((cols,)), dma((cols,)), dma((2,)), dma((2,)),
            dma((GROUP,)), dma((GROUP,)), dma((zs,)), dma((zs,)),
        ],
        compiler_params=pltpu.CompilerParams(collective_id=0, has_side_effects=True, vmem_limit_bytes=48 * 1024 * 1024),
    )(panel, materials, table, shifts, shift_pick)
    rows = cols * depth
    block = min(width, 512)
    tile = pl.BlockSpec((rows, block), lambda i: (0, i))
    basis = pl.pallas_call(
        functools.partial(apply_kernel, cols),
        name="apply",
        grid=(width // block,),
        out_shape=jax.ShapeDtypeStruct((rows, width), f32),
        in_specs=[pl.BlockSpec((2 * cols, LANES), lambda i: (0, 0)), tile, tile],
        out_specs=tile,
        scratch_shapes=[pltpu.VMEM((rows, LANES), jnp.bfloat16)] * 4,
    )(inv, w.reshape(rows, width), r.reshape(rows, width))
    return basis.reshape(cols, depth, width)


def solution(mesh):
    placed = (P("fac", "tile", None), P("tile", None), P(), P(), P())
    return jax.shard_map(
        functools.partial(per_device, mesh.shape["tile"]), mesh=mesh, in_specs=placed,
        out_specs=P("fac", "tile", None), check_vma=False,
    )
```

time: 603 us -> 62.5 us (0.10); the launches traced: 592 us -> 62.2 us
  blocking collectives: 501 us -> 0 us
  Pallas kernels: 0 us -> 56.2 us
  starting transfers between devices: 37.7 us -> 0 us
  waiting for transfers between devices: 28.4 us -> 0 us
  other arithmetic: 16.6 us -> 0 us
    psum x1 -> x0, blocking collectives: 501 us -> none  [per_device(): tile_sum = lax.psum(partial_value, 'tile')]
    pallas_call x0 -> x2, Pallas kernels: none -> 56.2 us  [the longest x1 51.5 us: per_device(): pl.pallas_call(functools.partial(solve_kernel, tiles), name='solve', out_...]
    ppermute x13 -> x0, starting transfers between devices: 37.7 us -> none  [the longest x5 22.8 us: padded(): before = lax.ppermute(last, axis, up)]
    ppermute x13 -> x0, waiting for transfers between devices: 28.4 us -> none  [the longest x3 20.5 us: swapped(): lax.ppermute(value, axis, [(i, i ^ 1 << apart) for i in range(lax.axis_si...]
    add x5 -> x0, other arithmetic: 6.78 us -> none  [the longest x4 6.47 us: relax(): return (1.0 - OMEGA) * center + OMEGA * (source + beside) * inverse]
    another operation x5 -> x0, other arithmetic: 6.68 us -> none  [the longest x3 3.6 us: per_device(): lower_factor = jnp.linalg.cholesky(total / ncells)]
  transfers between devices with their start and end apart: 13 -> 0, of which waited for: 8 -> 0; matrix products, arithmetic and copies ran while one was open for 0% -> 0% of each run, Pallas kernels for 0% -> 0%
where the time goes in v1:
time: 62.5 us; the launch traced here: 62.2 us
  Pallas kernels  56.2 us (90%)
  local copies, waits for them, and re-layouts  5.32 us (9%)
  between operations  0.7 us (1%)
    pallas_call x1, Pallas kernels, per_device(): pl.pallas_call(functools.partial(solve_kernel, tiles), name='solve', out_...  51.5 us
    unnamed x14, local copies, waits for them, and re-layouts  5.32 us
    pallas_call x1, Pallas kernels, per_device(): pl.pallas_call(functools.partial(apply_kernel, cols), name='apply', grid=...  4.7 us

profile of v1, /device:TPU:6, one launch (start us, length us, event | category | flops | bytes accessed | tf_op | source)
XLA Modules:
  0.0 62.2 jit_solution(696589871011523180)
XLA Ops:
  0.0 0.0 copy-start.6
  0.7 0.0 copy-done.6
  0.7 0.0 copy-start.2
  0.7 1.2 %copy-done.2 = f32[16,8,2048]{2,1,0:T(8,128)S(1)} copy-done((f32[16,8,2048]{2,1,0:T(8,128)S(1)}, f32[16,8,2048]{2,1,0:T(8,128)}, u32[]{:S(2)}) %copy-start.2) | copy-done | bytes 1048600
  1.9 0.0 copy-start.3
  1.9 0.8 %copy-done.3 = s32[8,2048]{1,0:T(8,128)S(1)} copy-done((s32[8,2048]{1,0:T(8,128)S(1)}, s32[8,2048]{1,0:T(8,128)}, u32[]{:S(2)}) %copy-start.3) | copy-done | bytes 65560
  2.7 0.0 copy-start.5
  2.7 0.7 %copy-done.5 = f32[4,8]{1,0:T(4,128)S(1)} copy-done((f32[4,8]{1,0:T(4,128)S(1)}, f32[4,8]{1,0:T(4,128)}, u32[]{:S(2)}) %copy-start.5) | copy-done | bytes 152
  3.4 51.5 %solve.1 = (f32[16,8,2048]{2,1,0:T(8,128)S(1)}, f32[16,8,2048]{2,1,0:T(8,128)S(1)}, f32[32,128]{1,0:T(8,128)S(1)}) custom-call(f32[16,8,2048]{2,1,0:T(8,128)S(1)} %copy-done.2, s32[8,2048]{1,0:T(8,128)S(1)} %copy-done.3, f32[4,8]{1,0:T(4,128)S(1)} %copy-done.5, f32[8]{0:T(128)S(1)} %copy-done.6, s32[1]{0:T(128)S(6)} %copy.6.pick), custom_call_target="tpu_custom_call" | custom-call | tf_op jit(solution)/shard_map/solve/pallas_call | solution.py:378
  54.9 0.0 copy-start
  54.9 1.0 %copy-done = f32[16,8,2048]{2,1,0:T(8,128)} copy-done((f32[16,8,2048]{2,1,0:T(8,128)}, f32[16,8,2048]{2,1,0:T(8,128)S(1)}, u32[]{:S(2)}) %copy-start) | copy-done | bytes 1048600
  55.9 0.0 copy-start.1
  55.9 1.0 %copy-done.1 = f32[16,8,2048]{2,1,0:T(8,128)} copy-done((f32[16,8,2048]{2,1,0:T(8,128)}, f32[16,8,2048]{2,1,0:T(8,128)S(1)}, u32[]{:S(2)}) %copy-start.1) | copy-done | bytes 1048600
  56.9 0.0 copy-start.4
  56.9 0.6 copy-done.4
  57.5 4.7 %apply.1 = f32[128,2048]{1,0:T(8,128)} custom-call(f32[32,128]{1,0:T(8,128)} %copy-done.4, f32[128,2048]{1,0:T(8,128)} %bitcast.3, f32[128,2048]{1,0:T(8,128)} %bitcast.4), custom_call_target="tpu_custom_call" | custom-call | tf_op jit(solution)/shard_map/apply/pallas_call | solution.py:402
Async XLA Ops:
  0.0 0.7 %copy-start.6 = (f32[8]{0:T(128)S(1)}, f32[8]{0:T(128)}, u32[]{:S(2)}) copy-start(f32[8]{0:T(128)} %shifts.1) | copy-start | bytes 100
  0.7 1.2 %copy-start.2 = (f32[16,8,2048]{2,1,0:T(8,128)S(1)}, f32[16,8,2048]{2,1,0:T(8,128)}, u32[]{:S(2)}) copy-start(f32[16,8,2048]{2,1,0:T(8,128)} %panel.1) | copy-start | bytes 3145732
  1.9 0.8 %copy-start.3 = (s32[8,2048]{1,0:T(8,128)S(1)}, s32[8,2048]{1,0:T(8,128)}, u32[]{:S(2)}) copy-start(s32[8,2048]{1,0:T(8,128)} %ids.1) | copy-start | bytes 196612
  2.7 0.7 %copy-start.5 = (f32[4,8]{1,0:T(4,128)S(1)}, f32[4,8]{1,0:T(4,128)}, u32[]{:S(2)}) copy-start(f32[4,8]{1,0:T(4,128)} %table.1) | copy-start | bytes 388
  54.9 1.0 %copy-start = (f32[16,8,2048]{2,1,0:T(8,128)}, f32[16,8,2048]{2,1,0:T(8,128)S(1)}, u32[]{:S(2)}) copy-start(f32[16,8,2048]{2,1,0:T(8,128)S(1)} %get-tuple-element.9) | copy-start | bytes 3145732
  55.9 1.0 %copy-start.1 = (f32[16,8,2048]{2,1,0:T(8,128)}, f32[16,8,2048]{2,1,0:T(8,128)S(1)}, u32[]{:S(2)}) copy-start(f32[16,8,2048]{2,1,0:T(8,128)S(1)} %get-tuple-element.10) | copy-start | bytes 3145732
  56.9 0.6 copy-start.4

commit v2 on v1

--- a/solution.py
+++ b/solution.py
@@ -152,8 +152,9 @@
     return pltpu.roll(scaled, LANES - size, 1)
 
 
-def solve_kernel(tiles, panel, ids, table, shifts, pick, w_out, r_out, inv_out, ext, idx, coef, inv_ref, w, r, gbuf, zbuf,
-                 ids_sem, own_sem, ids_send, ids_recv, halo_send, halo_recv, swap_send, swap_recv, rest_sem, out_sem,
+def solve_kernel(tiles, panel, ids, table_hbm, shifts_hbm, pick, w, r, inv_out, table, shifts,
+                 ext, idx, coef, inv_ref, gbuf, zbuf, token,
+                 scalar_sem, ids_sem, own_sem, ids_send, ids_recv, halo_send, halo_recv, swap_send, swap_recv, rest_sem,
                  group_send, group_recv, line_send, line_recv):
     cols = panel.shape[0]
     width = panel.shape[2]
@@ -169,10 +170,10 @@
     after = lax.rem(me + 1, tiles)
     seat = parity * LINE + spot
 
+    scalars = [pltpu.make_async_copy(a, b, scalar_sem.at[i])
+               for i, (a, b) in enumerate(((table_hbm, table), (shifts_hbm, shifts)))]
     own_ids = pltpu.make_async_copy(ids, idx.at[pl.ds(8, 8)], ids_sem)
-    own_ids.start()
     own_panel = pltpu.make_async_copy(panel, ext.at[:, pl.ds(HALO, 8)], own_sem)
-    own_panel.start()
 
     def group_peer(step):
         there = lax.rem(seat + step, GROUP)
@@ -183,17 +184,31 @@
         there = lax.rem(line + step, zs)
         return {"tile": there * LINE + spot, "fac": fac}, there
 
+    def along(distance):
+        return {"tile": lax.rem(line + distance + zs, zs) * LINE + spot, "fac": fac}
+
     barrier = pltpu.get_barrier_semaphore()
-    greeted = [{"tile": before, "fac": fac}, {"tile": after, "fac": fac}]
-    greeted += [group_peer(i)[0] for i in range(1, GROUP)]
-    greeted += [line_peer(i)[0] for i in range(1, zs)]
+    near = {"tile": me, "fac": partner}
+    greeted = [{"tile": before, "fac": fac}, {"tile": after, "fac": fac}, near]
+    greeted += [{"tile": line * LINE + lax.rem(spot + i, LINE), "fac": fac} for i in range(1, LINE)]
+    greeted += [along(i) for i in (-2, -1, 1, 2)]
     for peer in greeted:
         pl.semaphore_signal(barrier, inc=1, device_id=peer, device_id_type=MESH)
+    for copy in scalars + [own_ids, own_panel]:
+        copy.start()
     pl.semaphore_wait(barrier, len(greeted))
 
-    ids_up = pltpu.make_async_remote_copy(ids, idx.at[pl.ds(0, 8)], ids_send.at[0], ids_recv.at[0],
+    def greet(turn):
+        pl.semaphore_signal(token.at[2 * turn], inc=1, device_id=along(2), device_id_type=MESH)
+        pl.semaphore_signal(token.at[2 * turn + 1], inc=1, device_id=along(-2), device_id_type=MESH)
+
+    def greeted_by(turn):
+        pl.semaphore_wait(token.at[2 * turn], 1)
+        pl.semaphore_wait(token.at[2 * turn + 1], 1)
+
+    ids_up = pltpu.make_async_remote_copy(ids.at[pl.ds(3, 5)], idx.at[pl.ds(3, 5)], ids_send.at[0], ids_recv.at[0],
                                           device_id={"tile": after, "fac": fac}, device_id_type=MESH)
-    ids_down = pltpu.make_async_remote_copy(ids, idx.at[pl.ds(16, 8)], ids_send.at[1], ids_recv.at[1],
+    ids_down = pltpu.make_async_remote_copy(ids.at[pl.ds(0, 5)], idx.at[pl.ds(16, 5)], ids_send.at[1], ids_recv.at[1],
                                             device_id={"tile": before, "fac": fac}, device_id_type=MESH)
     ids_up.start()
     ids_down.start()
@@ -222,6 +237,10 @@
         return pltpu.make_async_remote_copy(w.at[c, :, giving], r.at[c, :, giving], swap_send.at[c], swap_recv.at[c],
                                             device_id={"tile": me, "fac": partner}, device_id_type=MESH)
 
+    pl.semaphore_signal(token.at[6], inc=1, device_id=near, device_id_type=MESH)
+    greet(0)
+    for copy in scalars:
+        copy.wait()
     shift_value = shifts[pick[0]]
     own_ids.wait()
     ids_up.wait()
@@ -237,6 +256,13 @@
         def _():
             swap(c - 1).start()
 
+        for turn in range(3):
+            @pl.when(c == 4 * (turn + 1))
+            def _():
+                greeted_by(turn)
+                if turn < 2:
+                    greet(turn + 1)
+
         values = solve_column(ext.at[c], coef, inv_ref)
         for k, value in enumerate(values):
             w[c, :, pl.ds(k * LANES, LANES)] = value[HALO:HALO + 8]
@@ -247,16 +273,12 @@
     gram = lax.dot_general(own, own, (((1,), (1,)), ((), ())), precision=HIGHEST, preferred_element_type=jnp.float32)
     swap(cols - 1).start()
     own_blocks = diagonal_blocks(gram)
-    keep_w = pltpu.make_async_copy(w, w_out, out_sem.at[0])
-    keep_w.start()
 
     def arrived(c, carry):
         swap(c).wait()
         return carry
 
     lax.fori_loop(0, cols, arrived, 0)
-    keep_r = pltpu.make_async_copy(r.at[:, :, getting], r_out.at[:, :, getting], out_sem.at[1])
-    keep_r.start()
     mine = w[:, :, getting].reshape(cols * 8, half)
     theirs = r[:, :, getting].reshape(cols * 8, half)
     cross = lax.dot_general(mine, theirs, (((1,), (1,)), ((), ())), precision=HIGHEST, preferred_element_type=jnp.float32)
@@ -286,9 +308,10 @@
         return pltpu.make_async_remote_copy(zbuf.at[there], zbuf.at[there], line_send.at[step], line_recv.at[there],
                                             device_id=peer, device_id_type=MESH)
 
-    rest = pltpu.make_async_remote_copy(w.at[:, :, pl.ds(half, half)], r_out.at[:, :, pl.ds(half, half)],
+    rest = pltpu.make_async_remote_copy(w.at[:, :, pl.ds(half, half)], r.at[:, :, pl.ds(half, half)],
                                         rest_sem.at[0], rest_sem.at[1],
                                         device_id={"tile": me, "fac": partner}, device_id_type=MESH)
+    pl.semaphore_wait(token.at[6], 1)
     for step in range(1, GROUP):
         group_copy(step).start()
 
@@ -317,8 +340,6 @@
         group_copy(step).wait_send()
     for step in range(1, zs):
         line_copy(step).wait_send()
-    keep_w.wait()
-    keep_r.wait()
 
     @pl.when(parity == 0)
     def _():
@@ -344,35 +365,50 @@
     return first + (second + third)
 
 
-def apply_kernel(cols, inv, w, r, out, own_high, own_low, rec_high, rec_low):
+def apply_kernel(cols, inv, w, r, out, stage, wide_high, wide_low, sems):
     parity = lax.axis_index("fac") % 2
-
-    @pl.when(pl.program_id(0) == 0)
+    size = cols * 8
+    width = w.shape[1]
+    block = width // 4
+    rows = jnp.where(parity == 0, inv[0:cols, :], inv[cols:2 * cols, :])
+    rows = jnp.broadcast_to(rows[:, None, :], (cols, 8, LANES)).reshape(size, LANES)
+    source = row_iota(LANES)
+    target = lane_iota(LANES)
+    same = (source % 8) == (target % 8)
+    for value, ref in zip(split(rows), (wide_high, wide_low)):
+        for part, first in ((0, parity * cols), (1, 0)):
+            spread = (source == first + target // 8).astype(jnp.bfloat16)
+            wide = jnp.dot(value, spread, preferred_element_type=jnp.float32)
+            ref[:, part * size:(part + 1) * size] = jnp.where(same, wide, 0.0).astype(jnp.bfloat16)
+
+    def send(k):
+        part = pl.ds(k * block, block)
+        return pltpu.make_async_copy(stage.at[:, part], out.at[:, part], sems.at[k])
+
+    @pl.when(parity == 0)
     def _():
-        rows = jnp.where(parity == 0, inv[0:cols, :], inv[cols:2 * cols, :])
-        rows = jnp.broadcast_to(rows[:, None, :], (cols, 8, LANES)).reshape(cols * 8, LANES)
-        high, low = split(rows)
-        source = row_iota(LANES)
-        target = lane_iota(LANES)
-        same = (source % 8) == (target % 8)
-        for first, ref_high, ref_low in ((parity * cols, own_high, own_low), (0, rec_high, rec_low)):
-            spread = (source == first + target // 8).astype(jnp.bfloat16)
-            for value, ref in ((high, ref_high), (low, ref_low)):
-                wide = jnp.dot(value, spread, preferred_element_type=jnp.float32)
-                ref[...] = jnp.where(same, wide, 0.0).astype(jnp.bfloat16)
-
-    out[...] = dot3((own_high[...], own_low[...]), split(w[...]))
+        for k in range(4):
+            part = pl.ds(k * block, block)
+            stage[:, part] = dot3((wide_high[:, 0:size], wide_low[:, 0:size]), split(w[:, part]))
+            send(k).start()
 
     @pl.when(parity == 1)
     def _():
-        out[...] += dot3((rec_high[...], rec_low[...]), split(r[...]))
+        for k in range(4):
+            part = pl.ds(k * block, block)
+            both = jnp.concatenate([w[:, part], r[:, part]], 0)
+            stage[:, part] = dot3((wide_high[...], wide_low[...]), split(both))
+            send(k).start()
+
+    for k in range(4):
+        send(k).wait()
 
 
 def per_device(tiles, panel, materials, table, shifts, shift_pick):
     cols, depth, width = panel.shape
     zs = tiles // LINE
-    anywhere = pl.BlockSpec(memory_space=pl.ANY)
-    scalars = pl.BlockSpec(memory_space=pltpu.SMEM)
+    hbm = pl.BlockSpec(memory_space=pltpu.HBM)
+    vmem = pl.BlockSpec(memory_space=pltpu.VMEM)
     dma = pltpu.SemaphoreType.DMA
     f32 = jnp.float32
     w, r, inv = pl.pallas_call(
@@ -380,33 +416,33 @@
         name="solve",
         out_shape=(jax.ShapeDtypeStruct((cols, depth, width), f32), jax.ShapeDtypeStruct((cols, depth, width), f32),
                    jax.ShapeDtypeStruct((2 * cols, LANES), f32)),
-        in_specs=[anywhere, anywhere, scalars, scalars, scalars],
-        out_specs=(anywhere, anywhere, pl.BlockSpec(memory_space=pltpu.VMEM)),
+        in_specs=[hbm] * 4 + [pl.BlockSpec(memory_space=pltpu.SMEM)],
+        out_specs=(vmem, vmem, vmem),
         scratch_shapes=[
+            pltpu.SMEM(table.shape, f32),
+            pltpu.SMEM(shifts.shape, f32),
             pltpu.VMEM((cols, 16, width), f32),
             pltpu.VMEM((24, width), jnp.int32),
             pltpu.VMEM((6, 16, width), f32),
             pltpu.VMEM((16, width), f32),
-            pltpu.VMEM((cols, depth, width), f32),
-            pltpu.VMEM((cols, depth, width), f32),
             pltpu.VMEM((GROUP, 8, LANES), f32),
             pltpu.VMEM((zs, 8, LANES), f32),
-            dma, dma, dma((2,)), dma((2,)), dma((2, cols)), dma((2, cols)), dma((cols,)), dma((cols,)), dma((2,)), dma((2,)),
+            pltpu.SemaphoreType.REGULAR((7,)),
+            dma((2,)), dma, dma, dma((2,)), dma((2,)), dma((2, cols)), dma((2, cols)), dma((cols,)), dma((cols,)), dma((2,)),
             dma((GROUP,)), dma((GROUP,)), dma((zs,)), dma((zs,)),
         ],
-        compiler_params=pltpu.CompilerParams(collective_id=0, has_side_effects=True, vmem_limit_bytes=48 * 1024 * 1024),
-    )(panel, materials, table, shifts, shift_pick)
+        compiler_params=pltpu.CompilerParams(collective_id=0, has_side_effects=True, vmem_limit_bytes=32 * 1024 * 1024),
+    )(*(pltpu.with_memory_space_constraint(a, pltpu.HBM) for a in (panel, materials, table, shifts)), shift_pick)
     rows = cols * depth
-    block = min(width, 512)
-    tile = pl.BlockSpec((rows, block), lambda i: (0, i))
     basis = pl.pallas_call(
         functools.partial(apply_kernel, cols),
         name="apply",
-        grid=(width // block,),
         out_shape=jax.ShapeDtypeStruct((rows, width), f32),
-        in_specs=[pl.BlockSpec((2 * cols, LANES), lambda i: (0, 0)), tile, tile],
-        out_specs=tile,
-        scratch_shapes=[pltpu.VMEM((rows, LANES), jnp.bfloat16)] * 4,
+        in_specs=[vmem] * 3,
+        out_specs=hbm,
+        scratch_shapes=[pltpu.VMEM((rows, width), f32), pltpu.VMEM((rows, 2 * rows), jnp.bfloat16),
+                        pltpu.VMEM((rows, 2 * rows), jnp.bfloat16), dma((4,))],
+        compiler_params=pltpu.CompilerParams(vmem_limit_bytes=32 * 1024 * 1024),
     )(inv, w.reshape(rows, width), r.reshape(rows, width))
     return basis.reshape(cols, depth, width)
 

time: 62.5 us -> 50 us (0.80)
  Pallas kernels: 56.2 us -> 49.2 us
  local copies, waits for them, and re-layouts: 5.32 us -> 0 us
    unnamed x14 -> x0, local copies, waits for them, and re-layouts: 5.32 us -> none
    pallas_call x1, Pallas kernels: 51.5 us -> 47.6 us  [per_device(): pl.pallas_call(functools.partial(solve_kernel, tiles), name='solve', out_...]
    pallas_call x1, Pallas kernels: 4.7 us -> 1.58 us  [per_device(): pl.pallas_call(functools.partial(apply_kernel, cols), name='apply', out_s...]
where the time goes in v2:
time: 50 us; the launch traced here: 49.8 us
  Pallas kernels  49.2 us (98%)
  between operations  0.66 us (1%)
    pallas_call x1, Pallas kernels, per_device(): pl.pallas_call(functools.partial(solve_kernel, tiles), name='solve', out_...  47.6 us
    pallas_call x1, Pallas kernels, per_device(): pl.pallas_call(functools.partial(apply_kernel, cols), name='apply', out_s...  1.58 us

profile of v2, /device:TPU:6, one launch (start us, length us, event | category | flops | bytes accessed | tf_op | source)
XLA Modules:
  0.0 49.8 jit_solution(8388726401886915696)
XLA Ops:
  0.7 47.6 %solve.1 = (f32[16,8,2048]{2,1,0:T(8,128)S(1)}, f32[16,8,2048]{2,1,0:T(8,128)S(1)}, f32[32,128]{1,0:T(8,128)S(1)}) custom-call(f32[16,8,2048]{2,1,0:T(8,128)} %panel.1, s32[8,2048]{1,0:T(8,128)} %ids.1, f32[4,8]{1,0:T(4,128)} %table_hbm.1, f32[8]{0:T(128)} %shifts_hbm.1, s32[1]{0:T(128)S(6)} %copy.6.pick), custom_call_target="tpu_custom_call" | custom-call | tf_op jit(solution)/shard_map/solve/pallas_call | solution.py:414
  48.3 1.6 %apply.1 = f32[128,2048]{1,0:T(8,128)} custom-call(f32[32,128]{1,0:T(8,128)S(1)} %get-tuple-element.8.inv, f32[128,2048]{1,0:T(8,128)S(1)} %bitcast.3, f32[128,2048]{1,0:T(8,128)S(1)} %bitcast.4), custom_call_target="tpu_custom_call" | custom-call | tf_op jit(solution)/shard_map/apply/pallas_call | solution.py:437

commit v3 on v2

--- a/solution.py
+++ b/solution.py
@@ -118,42 +118,63 @@
     return jnp.sum(kept.reshape(size // 8, 8, LANES), axis=1)
 
 
-def pack(blocks):
+def thirds(value):
+    parts = []
+    for _ in range(3):
+        part = value.astype(jnp.bfloat16)
+        parts.append(part)
+        value = value - part.astype(jnp.float32)
+    return jnp.concatenate(parts, 0)
+
+
+def pack(value, first_row, first_column):
     source = lax.broadcasted_iota(jnp.int32, (LANES, LANES), 0)
     target = lax.broadcasted_iota(jnp.int32, (LANES, LANES), 1)
-    left, right = [], []
-    for value, first_row, first_column in blocks:
-        for half in range(2):
-            left.append(value[half * 8:half * 8 + 8])
-            place = (first_row + half * 8) * 4 + first_column + source // 8
-            right.append((place == target).astype(jnp.float32))
-    total = None
-    for a, b in zip(left, right):
-        part = jnp.dot(a, b, precision=HIGHEST, preferred_element_type=jnp.float32)
-        total = part if total is None else total + part
-    return total
-
-
-def inverse_factor(packed, size):
+    places = []
+    for half in range(2):
+        place = (first_row + half * 8) * 4 + first_column + source // 8
+        places.append((place == target).astype(jnp.bfloat16))
+    left = jnp.concatenate([thirds(value[0:8]), thirds(value[8:16])], 1)
+    found = jnp.dot(left, jnp.concatenate(places, 0), preferred_element_type=jnp.float32)
+    return found[0:8] + (found[8:16] + found[16:24])
+
+
+def inverse_factor(packed, size, out):
+    count = size // 8
+    row = row_iota(8)
     lane = lane_iota(8)
-    eye_lane = lane_iota(size)
-    eye_row = row_iota(size)
-    tiles = [packed] + [pltpu.roll(packed, LANES - 32 * q, 1) for q in range(1, size // 8)]
-    matrix = jnp.concatenate([jnp.where(lane < size, t, 0.0) for t in tiles], 0)
-    matrix = jnp.where(eye_lane == eye_row + size, 1.0, matrix)
-    for k in range(size - 1):
-        row = matrix[k:k + 1, :]
-        column = matrix[:, k:k + 1]
-        pivot = 1.0 / matrix[k:k + 1, k:k + 1]
-        factor = jnp.where(eye_row > k, column * pivot, 0.0)
-        matrix = matrix - factor * row
-    diagonal = jnp.sum(jnp.where(eye_lane == eye_row, matrix, 0.0), axis=1, keepdims=True)
-    scaled = matrix * (1.0 / jnp.sqrt(diagonal))
-    return pltpu.roll(scaled, LANES - size, 1)
+
+    def spread(value, r):
+        return jnp.broadcast_to(value[r:r + 1, :], (8, LANES))
+
+    left = {(j, q): jnp.broadcast_to(packed[:, 32 * q + j:32 * q + j + 1], (8, LANES))
+            for j in range(size) for q in range(j // 8, count)}
+    right = [jnp.where(lane == row + 8 * q, 1.0, 0.0) for q in range(count)]
+    pivots = []
+    for k in range(size):
+        at, r = k // 8, k % 8
+        pivot = 1.0 / spread(left[k, at], r)
+        pivots.append(pivot)
+        if k == size - 1:
+            break
+        scaled = {q: left[k, q] * pivot for q in range(at, count)}
+        for j in range(k + 1, size):
+            other = spread(scaled[j // 8], j % 8)
+            for q in range(j // 8, count):
+                left[j, q] = left[j, q] - left[k, q] * other
+        source = spread(right[at], r)
+        for q in range(at, count):
+            factor = jnp.where(row > r, scaled[q], 0.0) if q == at else scaled[q]
+            right[q] = right[q] - factor * source
+    for q in range(count):
+        scale = pivots[8 * q]
+        for r in range(1, 8):
+            scale = jnp.where(row == r, pivots[8 * q + r], scale)
+        out[8 * q:8 * q + 8, :] = right[q] * jnp.sqrt(scale)
 
 
 def solve_kernel(tiles, panel, ids, table_hbm, shifts_hbm, pick, w, r, inv_out, table, shifts,
-                 ext, idx, coef, inv_ref, gbuf, zbuf, token,
+                 ext, idx, coef, inv_ref, cross, gbuf, zbuf, token,
                  scalar_sem, ids_sem, own_sem, ids_send, ids_recv, halo_send, halo_recv, swap_send, swap_recv, rest_sem,
                  group_send, group_recv, line_send, line_recv):
     cols = panel.shape[0]
@@ -272,7 +293,7 @@
     own = w[...].reshape(cols * 8, width)
     gram = lax.dot_general(own, own, (((1,), (1,)), ((), ())), precision=HIGHEST, preferred_element_type=jnp.float32)
     swap(cols - 1).start()
-    own_blocks = diagonal_blocks(gram)
+    own_packed = pack(diagonal_blocks(gram), parity * cols, parity * cols)
 
     def arrived(c, carry):
         swap(c).wait()
@@ -281,12 +302,19 @@
     lax.fori_loop(0, cols, arrived, 0)
     mine = w[:, :, getting].reshape(cols * 8, half)
     theirs = r[:, :, getting].reshape(cols * 8, half)
-    cross = lax.dot_general(mine, theirs, (((1,), (1,)), ((), ())), precision=HIGHEST, preferred_element_type=jnp.float32)
-    across = lax.dot_general(theirs, mine, (((1,), (1,)), ((), ())), precision=HIGHEST, preferred_element_type=jnp.float32)
-    mine_at = parity * cols
-    theirs_at = cols - mine_at
-    gbuf[seat] = pack([(own_blocks, mine_at, mine_at), (diagonal_blocks(cross), mine_at, theirs_at),
-                       (diagonal_blocks(across), theirs_at, mine_at)])
+
+    def product(a, b):
+        return lax.dot_general(a, b, (((1,), (1,)), ((), ())), precision=HIGHEST, preferred_element_type=jnp.float32)
+
+    @pl.when(parity == 0)
+    def _():
+        cross[...] = product(theirs, mine)
+
+    @pl.when(parity == 1)
+    def _():
+        cross[...] = product(mine, theirs)
+
+    gbuf[seat] = own_packed + pack(diagonal_blocks(cross[...]), cols, 0)
 
     def group_copy(step):
         peer, _ = group_peer(step)
@@ -334,7 +362,7 @@
     for i in range(1, zs):
         total = total + zbuf[i]
     cells = 8 * tiles * width
-    inv_out[...] = inverse_factor(total / cells, 2 * cols)
+    inverse_factor(total / cells, 2 * cols, inv_out)
 
     for step in range(1, GROUP):
         group_copy(step).wait_send()
@@ -357,15 +385,14 @@
 
 
 def dot3(a, b):
-    ah, al = a
-    bh, bl = b
-    first = jnp.dot(ah, bh, preferred_element_type=jnp.float32)
-    second = jnp.dot(ah, bl, preferred_element_type=jnp.float32)
-    third = jnp.dot(al, bh, preferred_element_type=jnp.float32)
-    return first + (second + third)
-
-
-def apply_kernel(cols, inv, w, r, out, stage, wide_high, wide_low, sems):
+    size = a.shape[0] // 2
+    high, low = split(b)
+    both = jnp.dot(a, high, preferred_element_type=jnp.float32)
+    rest = jnp.dot(a[0:size], low, preferred_element_type=jnp.float32)
+    return both[0:size] + (both[size:2 * size] + rest)
+
+
+def apply_kernel(cols, inv, w, r, out, stage, factor, sems):
     parity = lax.axis_index("fac") % 2
     size = cols * 8
     width = w.shape[1]
@@ -375,11 +402,12 @@
     source = row_iota(LANES)
     target = lane_iota(LANES)
     same = (source % 8) == (target % 8)
-    for value, ref in zip(split(rows), (wide_high, wide_low)):
-        for part, first in ((0, parity * cols), (1, 0)):
-            spread = (source == first + target // 8).astype(jnp.bfloat16)
-            wide = jnp.dot(value, spread, preferred_element_type=jnp.float32)
-            ref[:, part * size:(part + 1) * size] = jnp.where(same, wide, 0.0).astype(jnp.bfloat16)
+    rows = jnp.concatenate(split(rows), 0)
+    same = jnp.concatenate([same, same], 0)
+    for part, first in ((0, parity * cols), (1, 0)):
+        spread = (source == first + target // 8).astype(jnp.bfloat16)
+        wide = jnp.dot(rows, spread, preferred_element_type=jnp.float32)
+        factor[:, part * size:(part + 1) * size] = jnp.where(same, wide, 0.0).astype(jnp.bfloat16)
 
     def send(k):
         part = pl.ds(k * block, block)
@@ -389,7 +417,7 @@
     def _():
         for k in range(4):
             part = pl.ds(k * block, block)
-            stage[:, part] = dot3((wide_high[:, 0:size], wide_low[:, 0:size]), split(w[:, part]))
+            stage[:, part] = dot3(factor[:, 0:size], w[:, part])
             send(k).start()
 
     @pl.when(parity == 1)
@@ -397,7 +425,7 @@
         for k in range(4):
             part = pl.ds(k * block, block)
             both = jnp.concatenate([w[:, part], r[:, part]], 0)
-            stage[:, part] = dot3((wide_high[...], wide_low[...]), split(both))
+            stage[:, part] = dot3(factor[...], both)
             send(k).start()
 
     for k in range(4):
@@ -425,6 +453,7 @@
             pltpu.VMEM((24, width), jnp.int32),
             pltpu.VMEM((6, 16, width), f32),
             pltpu.VMEM((16, width), f32),
+            pltpu.VMEM((cols * depth, LANES), f32),
             pltpu.VMEM((GROUP, 8, LANES), f32),
             pltpu.VMEM((zs, 8, LANES), f32),
             pltpu.SemaphoreType.REGULAR((7,)),
@@ -440,8 +469,7 @@
         out_shape=jax.ShapeDtypeStruct((rows, width), f32),
         in_specs=[vmem] * 3,
         out_specs=hbm,
-        scratch_shapes=[pltpu.VMEM((rows, width), f32), pltpu.VMEM((rows, 2 * rows), jnp.bfloat16),
-                        pltpu.VMEM((rows, 2 * rows), jnp.bfloat16), dma((4,))],
+        scratch_shapes=[pltpu.VMEM((rows, width), f32), pltpu.VMEM((2 * rows, 2 * rows), jnp.bfloat16), dma((4,))],
         compiler_params=pltpu.CompilerParams(vmem_limit_bytes=32 * 1024 * 1024),
     )(inv, w.reshape(rows, width), r.reshape(rows, width))
     return basis.reshape(cols, depth, width)

time: 50 us -> 47.4 us (0.948)
  Pallas kernels: 49.2 us -> 46.6 us
    pallas_call x1, Pallas kernels: 47.6 us -> 45.1 us  [per_device(): pl.pallas_call(functools.partial(solve_kernel, tiles), name='solve', out_...]
where the time goes in v3:
time: 47.4 us; the launch traced here: 47.3 us
  Pallas kernels  46.6 us (98%)
  between operations  0.66 us (1%)
    pallas_call x1, Pallas kernels, per_device(): pl.pallas_call(functools.partial(solve_kernel, tiles), name='solve', out_...  45.1 us
    pallas_call x1, Pallas kernels, per_device(): pl.pallas_call(functools.partial(apply_kernel, cols), name='apply', out_s...  1.54 us

profile of v3, /device:TPU:6, one launch (start us, length us, event | category | flops | bytes accessed | tf_op | source)
XLA Modules:
  0.0 47.3 jit_solution(15085112627775567189)
XLA Ops:
  0.7 45.1 %solve.1 = (f32[16,8,2048]{2,1,0:T(8,128)S(1)}, f32[16,8,2048]{2,1,0:T(8,128)S(1)}, f32[32,128]{1,0:T(8,128)S(1)}) custom-call(f32[16,8,2048]{2,1,0:T(8,128)} %panel.1, s32[8,2048]{1,0:T(8,128)} %ids.1, f32[4,8]{1,0:T(4,128)} %table_hbm.1, f32[8]{0:T(128)} %shifts_hbm.1, s32[1]{0:T(128)S(6)} %copy.6.pick), custom_call_target="tpu_custom_call" | custom-call | tf_op jit(solution)/shard_map/solve/pallas_call | solution.py:442
  45.8 1.5 %apply.1 = f32[128,2048]{1,0:T(8,128)} custom-call(f32[32,128]{1,0:T(8,128)S(1)} %get-tuple-element.8.inv, f32[128,2048]{1,0:T(8,128)S(1)} %bitcast.3, f32[128,2048]{1,0:T(8,128)S(1)} %bitcast.4), custom_call_target="tpu_custom_call" | custom-call | tf_op jit(solution)/shard_map/apply/pallas_call | solution.py:466

commit v4 on v3

--- a/solution.py
+++ b/solution.py
@@ -175,7 +175,7 @@
 
 def solve_kernel(tiles, panel, ids, table_hbm, shifts_hbm, pick, w, r, inv_out, table, shifts,
                  ext, idx, coef, inv_ref, cross, gbuf, zbuf, token,
-                 scalar_sem, ids_sem, own_sem, ids_send, ids_recv, halo_send, halo_recv, swap_send, swap_recv, rest_sem,
+                 scalar_sem, ids_sem, own_sem, ids_send, ids_recv, halo_send, halo_recv, swap_send, swap_recv, rest_send, rest_recv,
                  group_send, group_recv, line_send, line_recv):
     cols = panel.shape[0]
     width = panel.shape[2]
@@ -252,7 +252,6 @@
     lax.fori_loop(0, cols, send_halo, 0)
 
     giving = pl.ds(pl.multiple_of(parity * half, half), half)
-    getting = pl.ds(pl.multiple_of((1 - parity) * half, half), half)
 
     def swap(c):
         return pltpu.make_async_remote_copy(w.at[c, :, giving], r.at[c, :, giving], swap_send.at[c], swap_recv.at[c],
@@ -290,29 +289,42 @@
         return carry
 
     lax.fori_loop(0, cols, column, 0)
+    def rest(part):
+        some = pl.ds(0, cols // 4) if part == 0 else pl.ds(cols // 4, cols - cols // 4)
+        side = pl.ds(half, half)
+        return pltpu.make_async_remote_copy(w.at[some, :, side], r.at[some, :, side], rest_send.at[part], rest_recv.at[part],
+                                            device_id=near, device_id_type=MESH)
+
     own = w[...].reshape(cols * 8, width)
     gram = lax.dot_general(own, own, (((1,), (1,)), ((), ())), precision=HIGHEST, preferred_element_type=jnp.float32)
     swap(cols - 1).start()
+
+    @pl.when(parity == 0)
+    def _():
+        rest(0).start()
+
     own_packed = pack(diagonal_blocks(gram), parity * cols, parity * cols)
 
     def arrived(c, carry):
         swap(c).wait()
         return carry
 
-    lax.fori_loop(0, cols, arrived, 0)
-    mine = w[:, :, getting].reshape(cols * 8, half)
-    theirs = r[:, :, getting].reshape(cols * 8, half)
-
     def product(a, b):
         return lax.dot_general(a, b, (((1,), (1,)), ((), ())), precision=HIGHEST, preferred_element_type=jnp.float32)
 
-    @pl.when(parity == 0)
-    def _():
-        cross[...] = product(theirs, mine)
-
-    @pl.when(parity == 1)
-    def _():
-        cross[...] = product(mine, theirs)
+    early = cols - cols // 4
+    for first, last in ((0, early), (early, cols)):
+        lax.fori_loop(first, last, arrived, 0)
+
+        @pl.when(parity == 0)
+        def _():
+            mine = w[:, :, half:].reshape(cols * 8, half)
+            cross[8 * first:8 * last, :] = product(r[first:last, :, half:].reshape((last - first) * 8, half), mine)
+
+        @pl.when(parity == 1)
+        def _():
+            mine = w[:, :, 0:half].reshape(cols * 8, half)
+            cross[:, 8 * first:8 * last] = product(mine, r[first:last, :, 0:half].reshape((last - first) * 8, half))
 
     gbuf[seat] = own_packed + pack(diagonal_blocks(cross[...]), cols, 0)
 
@@ -336,16 +348,13 @@
         return pltpu.make_async_remote_copy(zbuf.at[there], zbuf.at[there], line_send.at[step], line_recv.at[there],
                                             device_id=peer, device_id_type=MESH)
 
-    rest = pltpu.make_async_remote_copy(w.at[:, :, pl.ds(half, half)], r.at[:, :, pl.ds(half, half)],
-                                        rest_sem.at[0], rest_sem.at[1],
-                                        device_id={"tile": me, "fac": partner}, device_id_type=MESH)
     pl.semaphore_wait(token.at[6], 1)
     for step in range(1, GROUP):
         group_copy(step).start()
 
     @pl.when(parity == 0)
     def _():
-        rest.start()
+        rest(1).start()
 
     for step in range(1, GROUP):
         group_arrival(step).wait_recv()
@@ -371,11 +380,13 @@
 
     @pl.when(parity == 0)
     def _():
-        rest.wait_send()
+        rest(0).wait_send()
+        rest(1).wait_send()
 
     @pl.when(parity == 1)
     def _():
-        rest.wait_recv()
+        rest(0).wait_recv()
+        rest(1).wait_recv()
 
 
 def split(value):
@@ -457,7 +468,7 @@
             pltpu.VMEM((GROUP, 8, LANES), f32),
             pltpu.VMEM((zs, 8, LANES), f32),
             pltpu.SemaphoreType.REGULAR((7,)),
-            dma((2,)), dma, dma, dma((2,)), dma((2,)), dma((2, cols)), dma((2, cols)), dma((cols,)), dma((cols,)), dma((2,)),
+            dma((2,)), dma, dma, dma((2,)), dma((2,)), dma((2, cols)), dma((2, cols)), dma((cols,)), dma((cols,)), dma((2,)), dma((2,)),
             dma((GROUP,)), dma((GROUP,)), dma((zs,)), dma((zs,)),
         ],
         compiler_params=pltpu.CompilerParams(collective_id=0, has_side_effects=True, vmem_limit_bytes=32 * 1024 * 1024),

time: 47.4 us -> 46.7 us (0.985)
  Pallas kernels: 46.6 us -> 45.6 us
    pallas_call x1, Pallas kernels: 45.1 us -> 44 us  [per_device(): pl.pallas_call(functools.partial(solve_kernel, tiles), name='solve', out_...]
where the time goes in v4:
time: 46.7 us; the launch traced here: 46.2 us
  Pallas kernels  45.6 us (98%)
  between operations  0.66 us (1%)
    pallas_call x1, Pallas kernels, per_device(): pl.pallas_call(functools.partial(solve_kernel, tiles), name='solve', out_...  44 us
    pallas_call x1, Pallas kernels, per_device(): pl.pallas_call(functools.partial(apply_kernel, cols), name='apply', out_s...  1.54 us

profile of v4, /device:TPU:6, one launch (start us, length us, event | category | flops | bytes accessed | tf_op | source)
XLA Modules:
  0.0 46.2 jit_solution(1296450768530356134)
XLA Ops:
  0.7 44.0 %solve.1 = (f32[16,8,2048]{2,1,0:T(8,128)S(1)}, f32[16,8,2048]{2,1,0:T(8,128)S(1)}, f32[32,128]{1,0:T(8,128)S(1)}) custom-call(f32[16,8,2048]{2,1,0:T(8,128)} %panel.1, s32[8,2048]{1,0:T(8,128)} %ids.1, f32[4,8]{1,0:T(4,128)} %table_hbm.1, f32[8]{0:T(128)} %shifts_hbm.1, s32[1]{0:T(128)S(6)} %copy.6.pick), custom_call_target="tpu_custom_call" | custom-call | tf_op jit(solution)/shard_map/solve/pallas_call | solution.py:453
  44.7 1.5 %apply.1 = f32[128,2048]{1,0:T(8,128)} custom-call(f32[32,128]{1,0:T(8,128)S(1)} %get-tuple-element.8.inv, f32[128,2048]{1,0:T(8,128)S(1)} %bitcast.3, f32[128,2048]{1,0:T(8,128)S(1)} %bitcast.4), custom_call_target="tpu_custom_call" | custom-call | tf_op jit(solution)/shard_map/apply/pallas_call | solution.py:477

commit v5 on v4

--- a/solution.py
+++ b/solution.py
@@ -45,67 +45,100 @@
     return 2.0 * first * second / (first + second)
 
 
-def make_coefficients(tiles, me, shift_value, ids_ref, table, coef, inv_ref):
-    count = ids_ref.shape[1] // LANES
-    ids = chunked(ids_ref[...])
-    rows24 = row_iota(24)
-    cut = ((me == 0) & (rows24 == 7)) | ((me == tiles - 1) & (rows24 == 15))
-    lane = lane_iota(16)
+def plane_faces(ids, table, shift_value):
+    count = len(ids)
+    lane = lane_iota(8)
     left = lane < NZ
     top = (lane % NZ) == NZ - 1
-    cond_y = [pick_field(i[4:20], table, 1) for i in ids]
+    cond_y = [pick_field(i, table, 1) for i in ids]
     turned = [pltpu.roll(v, NZ, 1) for v in cond_y]
     faces_y = []
     for k in range(count):
         above = jnp.where(left, turned[k], turned[min(k + 1, count - 1)])
         face = harmonic(cond_y[k], above)
-        if k == count - 1:
-            face = jnp.where(left, face, 0.0)
-        faces_y.append(face)
+        faces_y.append(jnp.where(left, face, 0.0) if k == count - 1 else face)
     back_y = [pltpu.roll(v, NZ, 1) for v in faces_y]
+    found = []
     for k in range(count):
         below = back_y[k - 1] if k else jnp.zeros_like(back_y[0])
-        next_y = faces_y[k]
         prev_y = jnp.where(left, below, back_y[k])
-        cond_z = pick_field(ids[k][4:20], table, 2)
-        next_z = harmonic(cond_z, pltpu.roll(cond_z, LANES - 1, 1))
-        next_z = jnp.where(top, 0.0, next_z)
+        cond_z = pick_field(ids[k], table, 2)
+        next_z = jnp.where(top, 0.0, harmonic(cond_z, pltpu.roll(cond_z, LANES - 1, 1)))
         prev_z = pltpu.roll(next_z, 1, 1)
-        cond_x = pick_field(ids[k], table, 0)
-        faces_x = harmonic(cond_x, pltpu.roll(cond_x, 23, 0))
-        faces_x = jnp.where(cut, 0.0, faces_x)
-        prev_x = faces_x[3:19]
-        next_x = faces_x[4:20]
-        capacity = pick_field(ids[k][4:20], table, 3)
-        diagonal = shift_value * capacity + prev_x + next_x + prev_y + next_y + prev_z + next_z
-        inverse = 1.0 / diagonal
+        capacity = pick_field(ids[k], table, 3)
+        partial = shift_value * capacity + (prev_y + faces_y[k] + prev_z + next_z)
+        found.append((prev_y, faces_y[k], prev_z, next_z, partial))
+    return found
+
+
+def own_coefficients(shift_value, ids_ref, table, coef, inv_ref, cond_ref):
+    ids = chunked(ids_ref[0:8, :])
+    for k, (prev_y, next_y, prev_z, next_z, partial) in enumerate(plane_faces(ids, table, shift_value)):
+        where = pl.ds(k * LANES, LANES)
+        cond = pick_field(ids[k], table, 0)
+        coef[1, 0:8, where] = harmonic(cond, pltpu.roll(cond, 7, 0))
+        for i, face in enumerate((prev_y, next_y, prev_z, next_z)):
+            coef[2 + i, 0:8, where] = face
+        inv_ref[0:8, where] = partial
+        cond_ref[:, where] = cond
+
+
+def all_coefficients(tiles, me, shift_value, ids_ref, table, coef, inv_ref, cond_ref):
+    row = row_iota(8)
+    after = chunked(ids_ref[8:16, :])
+    before = chunked(ids_ref[16:24, :])
+    halo = plane_faces([jnp.where(row < HALO, a, b) for a, b in zip(after, before)], table, shift_value)
+    for k in range(len(after)):
+        where = pl.ds(k * LANES, LANES)
+        cond = cond_ref[:, where]
+        cond_after = pick_field(after[k], table, 0)
+        cond_before = pick_field(before[k], table, 0)
+        middle = jnp.where(row < HALO, cond_after, cond_before)
+        lower = jnp.where(row < HALO, pltpu.roll(cond_after, 1, 0), pltpu.roll(cond_before, 1, 0))
+        lower = jnp.where(row == 0, pltpu.roll(cond, 1, 0), lower)
+        upper = jnp.where(row < HALO, pltpu.roll(cond_after, 7, 0), pltpu.roll(cond_before, 7, 0))
+        upper = jnp.where(row == 7, pltpu.roll(cond, 7, 0), upper)
+        prev_halo = jnp.where((row == 0) & (me == tiles - 1), 0.0, harmonic(lower, middle))
+        next_halo = jnp.where((row == 7) & (me == 0), 0.0, harmonic(middle, upper))
+        inner = coef[1, 0:8, where]
+        next_own = jnp.where(row == 7, pltpu.roll(prev_halo, 7, 0), inner)
+        prev_own = jnp.where(row == 0, pltpu.roll(next_halo, 1, 0), pltpu.roll(inner, 1, 0))
+        inverse = 1.0 / (inv_ref[0:8, where] + (prev_own + next_own))
         scaled = OMEGA * inverse
-        where = pl.ds(k * LANES, LANES)
-        for i, face in enumerate((prev_x, next_x, prev_y, next_y, prev_z, next_z)):
-            coef[i, :, where] = face * scaled
-        inv_ref[:, where] = inverse
+        coef[0, 0:8, where] = prev_own * scaled
+        coef[1, 0:8, where] = next_own * scaled
+        for i in range(2, 6):
+            coef[i, 0:8, where] = coef[i, 0:8, where] * scaled
+        inv_ref[0:8, where] = inverse
+        inverse = 1.0 / (halo[k][4] + (prev_halo + next_halo))
+        scaled = OMEGA * inverse
+        for i, face in enumerate((prev_halo, next_halo) + halo[k][0:4]):
+            coef[i, 8:16, where] = face * scaled
+        inv_ref[8:16, where] = inverse
 
 
 def solve_column(source_ref, coef, inv_ref):
     count = inv_ref.shape[1] // LANES
     where = [pl.ds(k * LANES, LANES) for k in range(count)]
-    left = lane_iota(16) < NZ
     values = [source_ref[:, where[k]] * inv_ref[:, where[k]] for k in range(count)]
     base = [OMEGA * v for v in values]
     for sweep in range(SWEEPS):
-        turned = [pltpu.roll(v, NZ, 1) for v in values]
+        rows = 8 if sweep == SWEEPS - 1 else 16
+        left = lane_iota(rows) < NZ
+        centers = [v[0:rows] for v in values]
+        turned = [pltpu.roll(v, NZ, 1) for v in centers]
         new = []
         for k in range(count):
-            v = values[k]
-            total = (1.0 - OMEGA) * v + base[k]
-            total += coef[0, :, where[k]] * pltpu.roll(v, 1, 0)
-            total += coef[1, :, where[k]] * pltpu.roll(v, 15, 0)
+            v = centers[k]
+            total = (1.0 - OMEGA) * v + base[k][0:rows]
+            total += coef[0, 0:rows, where[k]] * pltpu.roll(values[k], 1, 0)[0:rows]
+            total += coef[1, 0:rows, where[k]] * pltpu.roll(values[k], 15, 0)[0:rows]
             below = jnp.where(left, turned[max(k - 1, 0)], turned[k])
             above = jnp.where(left, turned[k], turned[min(k + 1, count - 1)])
-            total += coef[2, :, where[k]] * below
-            total += coef[3, :, where[k]] * above
-            total += coef[4, :, where[k]] * pltpu.roll(v, 1, 1)
-            total += coef[5, :, where[k]] * pltpu.roll(v, LANES - 1, 1)
+            total += coef[2, 0:rows, where[k]] * below
+            total += coef[3, 0:rows, where[k]] * above
+            total += coef[4, 0:rows, where[k]] * pltpu.roll(v, 1, 1)
+            total += coef[5, 0:rows, where[k]] * pltpu.roll(v, LANES - 1, 1)
             new.append(total)
         values = new
     return values
@@ -174,7 +207,7 @@
 
 
 def solve_kernel(tiles, panel, ids, table_hbm, shifts_hbm, pick, w, r, inv_out, table, shifts,
-                 ext, idx, coef, inv_ref, cross, gbuf, zbuf, token,
+                 ext, idx, coef, inv_ref, cond, cross, gbuf, zbuf, token,
                  scalar_sem, ids_sem, own_sem, ids_send, ids_recv, halo_send, halo_recv, swap_send, swap_recv, rest_send, rest_recv,
                  group_send, group_recv, line_send, line_recv):
     cols = panel.shape[0]
@@ -193,13 +226,17 @@
 
     scalars = [pltpu.make_async_copy(a, b, scalar_sem.at[i])
                for i, (a, b) in enumerate(((table_hbm, table), (shifts_hbm, shifts)))]
-    own_ids = pltpu.make_async_copy(ids, idx.at[pl.ds(8, 8)], ids_sem)
-    own_panel = pltpu.make_async_copy(panel, ext.at[:, pl.ds(HALO, 8)], own_sem)
+    own_ids = pltpu.make_async_copy(ids, idx.at[pl.ds(0, 8)], ids_sem)
 
     def group_peer(step):
-        there = lax.rem(seat + step, GROUP)
-        peer_fac = fac - parity + there // LINE
-        return {"tile": line * LINE + there % LINE, "fac": peer_fac}, there
+        core = lax.rem(spot % CORES + step % CORES, CORES)
+        y = lax.rem(spot // CORES + step // CORES % YS, YS)
+        x = lax.rem(parity + step // LINE, 2)
+        return {"tile": line * LINE + y * CORES + core, "fac": fac - parity + x}, x * LINE + y * CORES + core
+
+    def group_distance(step):
+        y = step // CORES % YS
+        return step // LINE + min(y, YS - y) + 0.5 * (step % CORES)
 
     def line_peer(step):
         there = lax.rem(line + step, zs)
@@ -215,7 +252,7 @@
     greeted += [along(i) for i in (-2, -1, 1, 2)]
     for peer in greeted:
         pl.semaphore_signal(barrier, inc=1, device_id=peer, device_id_type=MESH)
-    for copy in scalars + [own_ids, own_panel]:
+    for copy in scalars + [own_ids]:
         copy.start()
     pl.semaphore_wait(barrier, len(greeted))
 
@@ -227,26 +264,30 @@
         pl.semaphore_wait(token.at[2 * turn], 1)
         pl.semaphore_wait(token.at[2 * turn + 1], 1)
 
-    ids_up = pltpu.make_async_remote_copy(ids.at[pl.ds(3, 5)], idx.at[pl.ds(3, 5)], ids_send.at[0], ids_recv.at[0],
+    ids_up = pltpu.make_async_remote_copy(ids.at[pl.ds(3, 5)], idx.at[pl.ds(19, 5)], ids_send.at[0], ids_recv.at[0],
                                           device_id={"tile": after, "fac": fac}, device_id_type=MESH)
-    ids_down = pltpu.make_async_remote_copy(ids.at[pl.ds(0, 5)], idx.at[pl.ds(16, 5)], ids_send.at[1], ids_recv.at[1],
+    ids_down = pltpu.make_async_remote_copy(ids.at[pl.ds(0, 5)], idx.at[pl.ds(8, 5)], ids_send.at[1], ids_recv.at[1],
                                             device_id={"tile": before, "fac": fac}, device_id_type=MESH)
     ids_up.start()
     ids_down.start()
 
     def halo_up(c):
-        return pltpu.make_async_remote_copy(panel.at[c, pl.ds(8 - HALO, HALO)], ext.at[c, pl.ds(0, HALO)],
+        return pltpu.make_async_remote_copy(panel.at[c, pl.ds(8 - HALO, HALO)], ext.at[c, pl.ds(8 + HALO, HALO)],
                                             halo_send.at[0, c], halo_recv.at[0, c],
                                             device_id={"tile": after, "fac": fac}, device_id_type=MESH)
 
     def halo_down(c):
-        return pltpu.make_async_remote_copy(panel.at[c, pl.ds(0, HALO)], ext.at[c, pl.ds(8 + HALO, HALO)],
+        return pltpu.make_async_remote_copy(panel.at[c, pl.ds(0, HALO)], ext.at[c, pl.ds(8, HALO)],
                                             halo_send.at[1, c], halo_recv.at[1, c],
                                             device_id={"tile": before, "fac": fac}, device_id_type=MESH)
+
+    def own_column(c):
+        return pltpu.make_async_copy(panel.at[c], ext.at[c, pl.ds(0, 8)], own_sem.at[c])
 
     def send_halo(c, carry):
         halo_up(c).start()
         halo_down(c).start()
+        own_column(c).start()
         return carry
 
     lax.fori_loop(0, cols, send_halo, 0)
@@ -263,14 +304,15 @@
         copy.wait()
     shift_value = shifts[pick[0]]
     own_ids.wait()
+    own_coefficients(shift_value, idx, table, coef, inv_ref, cond)
     ids_up.wait()
     ids_down.wait()
-    make_coefficients(tiles, me, shift_value, idx, table, coef, inv_ref)
-    own_panel.wait()
+    all_coefficients(tiles, me, shift_value, idx, table, coef, inv_ref, cond)
 
     def column(c, carry):
         halo_up(c).wait()
         halo_down(c).wait()
+        own_column(c).wait()
 
         @pl.when(c > 0)
         def _():
@@ -285,7 +327,7 @@
 
         values = solve_column(ext.at[c], coef, inv_ref)
         for k, value in enumerate(values):
-            w[c, :, pl.ds(k * LANES, LANES)] = value[HALO:HALO + 8]
+            w[c, :, pl.ds(k * LANES, LANES)] = value
         return carry
 
     lax.fori_loop(0, cols, column, 0)
@@ -349,7 +391,7 @@
                                             device_id=peer, device_id_type=MESH)
 
     pl.semaphore_wait(token.at[6], 1)
-    for step in range(1, GROUP):
+    for step in sorted(range(1, GROUP), key=group_distance, reverse=True):
         group_copy(step).start()
 
     @pl.when(parity == 0)
@@ -464,11 +506,12 @@
             pltpu.VMEM((24, width), jnp.int32),
             pltpu.VMEM((6, 16, width), f32),
             pltpu.VMEM((16, width), f32),
+            pltpu.VMEM((8, width), f32),
             pltpu.VMEM((cols * depth, LANES), f32),
             pltpu.VMEM((GROUP, 8, LANES), f32),
             pltpu.VMEM((zs, 8, LANES), f32),
             pltpu.SemaphoreType.REGULAR((7,)),
-            dma((2,)), dma, dma, dma((2,)), dma((2,)), dma((2, cols)), dma((2, cols)), dma((cols,)), dma((cols,)), dma((2,)), dma((2,)),
+            dma((2,)), dma, dma((cols,)), dma((2,)), dma((2,)), dma((2, cols)), dma((2, cols)), dma((cols,)), dma((cols,)), dma((2,)), dma((2,)),
             dma((GROUP,)), dma((GROUP,)), dma((zs,)), dma((zs,)),
         ],
         compiler_params=pltpu.CompilerParams(collective_id=0, has_side_effects=True, vmem_limit_bytes=32 * 1024 * 1024),

time: 46.7 us -> 46.5 us (level)
  no operation moved by 1% of the time
where the time goes in v5:
time: 46.5 us; the launch traced here: 46 us
  Pallas kernels  45.4 us (98%)
  between operations  0.66 us (1%)
    pallas_call x1, Pallas kernels, per_device(): pl.pallas_call(functools.partial(solve_kernel, tiles), name='solve', out_...  43.8 us
    pallas_call x1, Pallas kernels, per_device(): pl.pallas_call(functools.partial(apply_kernel, cols), name='apply', out_s...  1.54 us

profile of v5, /device:TPU:6, one launch (start us, length us, event | category | flops | bytes accessed | tf_op | source)
XLA Modules:
  0.0 46.0 jit_solution(3310954117544165764)
XLA Ops:
  0.7 43.8 %solve.1 = (f32[16,8,2048]{2,1,0:T(8,128)S(1)}, f32[16,8,2048]{2,1,0:T(8,128)S(1)}, f32[32,128]{1,0:T(8,128)S(1)}) custom-call(f32[16,8,2048]{2,1,0:T(8,128)} %panel.1, s32[8,2048]{1,0:T(8,128)} %ids.1, f32[4,8]{1,0:T(4,128)} %table_hbm.1, f32[8]{0:T(128)} %shifts_hbm.1, s32[1]{0:T(128)S(6)} %copy.6.pick), custom_call_target="tpu_custom_call" | custom-call | tf_op jit(solution)/shard_map/solve/pallas_call | solution.py:495
  44.5 1.5 %apply.1 = f32[128,2048]{1,0:T(8,128)} custom-call(f32[32,128]{1,0:T(8,128)S(1)} %get-tuple-element.8.inv, f32[128,2048]{1,0:T(8,128)S(1)} %bitcast.3, f32[128,2048]{1,0:T(8,128)S(1)} %bitcast.4), custom_call_target="tpu_custom_call" | custom-call | tf_op jit(solution)/shard_map/apply/pallas_call | solution.py:520

commit v6 on v5

--- a/solution.py
+++ b/solution.py
@@ -391,19 +391,40 @@
                                             device_id=peer, device_id_type=MESH)
 
     pl.semaphore_wait(token.at[6], 1)
-    for step in sorted(range(1, GROUP), key=group_distance, reverse=True):
-        group_copy(step).start()
+
+    def outward(steps):
+        return sorted(steps, key=group_distance, reverse=True)
 
     @pl.when(parity == 0)
     def _():
+        for step in outward(range(1, GROUP)):
+            group_copy(step).start()
         rest(1).start()
 
-    for step in range(1, GROUP):
+    @pl.when(parity == 1)
+    def _():
+        for step in outward(range(1, LINE)):
+            group_copy(step).start()
+
+    for step in range(1, LINE):
         group_arrival(step).wait_recv()
-    total = gbuf[0]
-    for i in range(1, GROUP):
-        total = total + gbuf[i]
-    zbuf[line] = total
+
+    def group_sum(count):
+        total = gbuf[0]
+        for i in range(1, count):
+            total = total + gbuf[i]
+        zbuf[line] = total
+
+    @pl.when(parity == 0)
+    def _():
+        group_sum(LINE)
+
+    @pl.when(parity == 1)
+    def _():
+        for step in range(LINE, GROUP):
+            group_arrival(step).wait_recv()
+        group_sum(GROUP)
+
     order = sorted(range(1, zs), key=lambda s: -min(s, zs - s))
     for step in order:
         line_copy(step).start()
@@ -413,15 +434,24 @@
     for i in range(1, zs):
         total = total + zbuf[i]
     cells = 8 * tiles * width
-    inverse_factor(total / cells, 2 * cols, inv_out)
-
-    for step in range(1, GROUP):
+
+    @pl.when(parity == 0)
+    def _():
+        inverse_factor(total / cells, cols, inv_out)
+
+    @pl.when(parity == 1)
+    def _():
+        inverse_factor(total / cells, 2 * cols, inv_out)
+
+    for step in range(1, LINE):
         group_copy(step).wait_send()
     for step in range(1, zs):
         line_copy(step).wait_send()
 
     @pl.when(parity == 0)
     def _():
+        for step in range(LINE, GROUP):
+            group_copy(step).wait_send()
         rest(0).wait_send()
         rest(1).wait_send()
 

time: 46.5 us -> 46.1 us (level)
  no operation moved by 1% of the time
where the time goes in v6:
time: 46.1 us; the launch traced here: 46 us
  Pallas kernels  45.4 us (98%)
  between operations  0.66 us (1%)
    pallas_call x1, Pallas kernels, per_device(): pl.pallas_call(functools.partial(solve_kernel, tiles), name='solve', out_...  43.8 us
    pallas_call x1, Pallas kernels, per_device(): pl.pallas_call(functools.partial(apply_kernel, cols), name='apply', out_s...  1.54 us

profile of v6, /device:TPU:6, one launch (start us, length us, event | category | flops | bytes accessed | tf_op | source)
XLA Modules:
  0.0 46.0 jit_solution(15713914243333251565)
XLA Ops:
  0.7 43.8 %solve.1 = (f32[16,8,2048]{2,1,0:T(8,128)S(1)}, f32[16,8,2048]{2,1,0:T(8,128)S(1)}, f32[32,128]{1,0:T(8,128)S(1)}) custom-call(f32[16,8,2048]{2,1,0:T(8,128)} %panel.1, s32[8,2048]{1,0:T(8,128)} %ids.1, f32[4,8]{1,0:T(4,128)} %table_hbm.1, f32[8]{0:T(128)} %shifts_hbm.1, s32[1]{0:T(128)S(6)} %copy.6.pick), custom_call_target="tpu_custom_call" | custom-call | tf_op jit(solution)/shard_map/solve/pallas_call | solution.py:525
  44.5 1.5 %apply.1 = f32[128,2048]{1,0:T(8,128)} custom-call(f32[32,128]{1,0:T(8,128)S(1)} %get-tuple-element.8.inv, f32[128,2048]{1,0:T(8,128)S(1)} %bitcast.3, f32[128,2048]{1,0:T(8,128)S(1)} %bitcast.4), custom_call_target="tpu_custom_call" | custom-call | tf_op jit(solution)/shard_map/apply/pallas_call | solution.py:550

commit v7 on v6

--- a/solution.py
+++ b/solution.py
@@ -393,7 +393,7 @@
     pl.semaphore_wait(token.at[6], 1)
 
     def outward(steps):
-        return sorted(steps, key=group_distance, reverse=True)
+        return sorted(steps, key=lambda step: (step >= LINE, group_distance(step)), reverse=True)
 
     @pl.when(parity == 0)
     def _():

time: 46.1 us -> 46.1 us (level)
  no operation moved by 1% of the time
where the time goes in v7:
time: 46.1 us; the launch traced here: 46 us
  Pallas kernels  45.4 us (98%)
  between operations  0.66 us (1%)
    pallas_call x1, Pallas kernels, per_device(): pl.pallas_call(functools.partial(solve_kernel, tiles), name='solve', out_...  43.8 us
    pallas_call x1, Pallas kernels, per_device(): pl.pallas_call(functools.partial(apply_kernel, cols), name='apply', out_s...  1.54 us

profile of v7, /device:TPU:6, one launch (start us, length us, event | category | flops | bytes accessed | tf_op | source)
XLA Modules:
  0.0 46.0 jit_solution(15023594870418491561)
XLA Ops:
  0.7 43.8 %solve.1 = (f32[16,8,2048]{2,1,0:T(8,128)S(1)}, f32[16,8,2048]{2,1,0:T(8,128)S(1)}, f32[32,128]{1,0:T(8,128)S(1)}) custom-call(f32[16,8,2048]{2,1,0:T(8,128)} %panel.1, s32[8,2048]{1,0:T(8,128)} %ids.1, f32[4,8]{1,0:T(4,128)} %table_hbm.1, f32[8]{0:T(128)} %shifts_hbm.1, s32[1]{0:T(128)S(6)} %copy.6.pick), custom_call_target="tpu_custom_call" | custom-call | tf_op jit(solution)/shard_map/solve/pallas_call | solution.py:525
  44.5 1.5 %apply.1 = f32[128,2048]{1,0:T(8,128)} custom-call(f32[32,128]{1,0:T(8,128)S(1)} %get-tuple-element.8.inv, f32[128,2048]{1,0:T(8,128)S(1)} %bitcast.3, f32[128,2048]{1,0:T(8,128)S(1)} %bitcast.4), custom_call_target="tpu_custom_call" | custom-call | tf_op jit(solution)/shard_map/apply/pallas_call | solution.py:550
